TPU v7x, 512 devices: a whole 4x4x16 slice. The times are simulated.
512 devices in a mesh: seq: 128 (over y, z, core), ch: 4 (over x).
Axes of the slice: x: 4, y: 4, z: 16, core: 2. Of those that a mesh axis runs over, the one named last changes fastest.
Arguments:
- qkv: bfloat16 [3, 16384, 2048], P(None, 'seq', 'ch'), may hold values from -6 to 6
- filt: float32 [16384, 2048], P('seq', 'ch'), may hold values from -0.1875 to 0.1875
- skip_gain: float32 [2048], P('ch'), may hold values from -4 to 4
- short_weight: float32 [3, 3, 2048], P(None, None, 'ch'), may hold values from -3.5 to 3.5
- w_out: bfloat16 [2048, 2048], P(None, 'ch'), may hold values from -0.125 to 0.125
- g_out: bfloat16 [16384, 2048], P('seq', 'ch'), may hold values from -6 to 6
Outputs:
- output: bfloat16 [16384, 2048], P('seq', 'ch')
- grad_qkv: bfloat16 [3, 16384, 2048], P(None, 'seq', 'ch')
- grad_filter: float32 [16384, 2048], P('seq', 'ch')
All inputs are finite; a program needn't handle non-finite values.
Results may differ from a plain program's by a relative error of at most 0.0049.
Values may be sent and summed in bfloat16 or wider, within the bound.
A program may use at most 64 MiB of HBM per device.

v0:
```python
import math
import jax
import jax.numpy as jnp
from jax import lax
from jax.sharding import PartitionSpec as P

HIGHEST = lax.Precision.HIGHEST
TWO_PI = 2.0 * math.pi


def passed_along(block, axis, distance):
    devices = range(lax.axis_size(axis))
    route = [(i - distance, i) for i in devices if i - distance in devices]
    return lax.ppermute(block, axis, route)


def phase_pair(left_count, right_count, period, left_start, right_start):
    left_idx = lax.broadcasted_iota(jnp.int32, (left_count, right_count), 0) + left_start
    right_idx = lax.broadcasted_iota(jnp.int32, (left_count, right_count), 1) + right_start
    angle_all = (left_idx * right_idx % period).astype(jnp.float32) * (TWO_PI / period)
    return (jnp.cos(angle_all), jnp.sin(angle_all))


def contract(pattern, matrix, values):
    return jnp.einsum(
        pattern, matrix, values, precision=HIGHEST, preferred_element_type=jnp.float32
    )


def forward_spectrum(signal):
    seq_parts = lax.axis_size("seq")
    row_count = signal.shape[0]
    row_share = row_count // seq_parts
    period = 2 * seq_parts * row_count
    spread_in = lax.all_to_all(signal[None], "seq", split_axis=1, concat_axis=0, tiled=True)
    outer_cos, outer_sin = phase_pair(2 * seq_parts, seq_parts, 2 * seq_parts, 0, 0)
    section_re = contract("cp,prw->crw", outer_cos, spread_in)
    section_im = -contract("cp,prw->crw", outer_sin, spread_in)
    twist_cos, twist_sin = phase_pair(
        2 * seq_parts, row_share, period, 0, lax.axis_index("seq") * row_share
    )
    twist_cos = twist_cos[:, :, None]
    twist_sin = twist_sin[:, :, None]
    turned_re = section_re * twist_cos + section_im * twist_sin
    turned_im = section_im * twist_cos - section_re * twist_sin
    inner_cos, inner_sin = phase_pair(row_count, row_count, row_count, 0, 0)
    piece_re = lax.all_to_all(turned_re, "seq", split_axis=0, concat_axis=1, tiled=True)
    piece_im = lax.all_to_all(turned_im, "seq", split_axis=0, concat_axis=1, tiled=True)
    spec_re = contract("dm,cmk->cdk", inner_cos, piece_re) + contract(
        "dm,cmk->cdk", inner_sin, piece_im
    )
    spec_im = contract("dm,cmk->cdk", inner_cos, piece_im) - contract(
        "dm,cmk->cdk", inner_sin, piece_re
    )
    return (spec_re, spec_im)


def time_signal(spec_re, spec_im):
    seq_parts = lax.axis_size("seq")
    row_count = spec_re.shape[1]
    period = 2 * seq_parts * row_count
    inner_cos, inner_sin = phase_pair(row_count, row_count, row_count, 0, 0)
    back_re = contract("md,cdk->cmk", inner_cos, spec_re) - contract(
        "md,cdk->cmk", inner_sin, spec_im
    )
    back_im = contract("md,cdk->cmk", inner_cos, spec_im) + contract(
        "md,cdk->cmk", inner_sin, spec_re
    )
    twist_cos, twist_sin = phase_pair(2, row_count, period, 2 * lax.axis_index("seq"), 0)
    twist_cos = twist_cos[:, :, None]
    twist_sin = twist_sin[:, :, None]
    turned_re = back_re * twist_cos - back_im * twist_sin
    turned_im = back_im * twist_cos + back_re * twist_sin
    outer_cos, outer_sin = phase_pair(seq_parts, 2 * seq_parts, 2 * seq_parts, 0, 0)
    piece_re = lax.all_to_all(turned_re, "seq", split_axis=1, concat_axis=0, tiled=True)
    piece_im = lax.all_to_all(turned_im, "seq", split_axis=1, concat_axis=0, tiled=True)
    summed = contract("pc,crk->prk", outer_cos, piece_re) - contract(
        "pc,crk->prk", outer_sin, piece_im
    )
    returned = summed * (1.0 / period)
    return lax.all_to_all(returned, "seq", split_axis=0, concat_axis=1, tiled=True)[0]


def local(qkv, filt, skip_gain, short_weight, w_out, g_out):
    row_count = qkv.shape[1]
    slab_width = qkv.shape[2]
    tail_rows = passed_along(qkv[:, row_count - 2 :, :], "seq", 1)
    extended = jnp.concatenate([tail_rows, qkv], axis=1)
    short = (
        short_weight[:, 0, None, :] * extended[:, 2:, :]
        + short_weight[:, 1, None, :] * extended[:, 1:-1, :]
        + short_weight[:, 2, None, :] * extended[:, :-2, :]
    )
    query_gate = short[0]
    key_short = short[1]
    value_short = short[2]
    mixed = key_short * value_short
    both_re, both_im = forward_spectrum(jnp.concatenate([mixed, filt], axis=1))
    signal_re = both_re[:, :, :slab_width]
    signal_im = both_im[:, :, :slab_width]
    kernel_re = both_re[:, :, slab_width:]
    kernel_im = both_im[:, :, slab_width:]
    conv_out = time_signal(
        signal_re * kernel_re - signal_im * kernel_im, signal_re * kernel_im + signal_im * kernel_re
    )
    long_out = conv_out + skip_gain * mixed
    gated_out = (query_gate * long_out).astype(jnp.bfloat16)
    projected = jnp.dot(
        lax.all_gather(gated_out, "ch", axis=1, tiled=True),
        w_out,
        preferred_element_type=jnp.float32,
    )
    output = projected.astype(jnp.bfloat16)
    grad_all = lax.all_gather(g_out, "ch", axis=1, tiled=True)
    rows_all = lax.all_to_all(w_out, "ch", split_axis=0, concat_axis=1, tiled=True)
    grad_gated = lax.dot_general(
        grad_all, rows_all, (((1,), (1,)), ((), ())), preferred_element_type=jnp.float32
    )
    grad_long = grad_gated * query_gate
    grad_query = grad_gated * long_out
    grad_re, grad_im = forward_spectrum(grad_long)
    pair_re = jnp.concatenate(
        [kernel_re * grad_re + kernel_im * grad_im, signal_re * grad_re + signal_im * grad_im],
        axis=2,
    )
    pair_im = jnp.concatenate(
        [kernel_re * grad_im - kernel_im * grad_re, signal_re * grad_im - signal_im * grad_re],
        axis=2,
    )
    pair_time = time_signal(pair_re, pair_im)
    grad_mixed = pair_time[:, :slab_width] + skip_gain * grad_long
    token_total = lax.axis_size("seq") * row_count
    grad_filter = pair_time[:, slab_width:] * (1.0 / math.sqrt(token_total))
    grad_short = jnp.stack([grad_query, grad_mixed * value_short, grad_mixed * key_short])
    head_rows = passed_along(grad_short[:, :2, :], "seq", -1)
    extended_grad = jnp.concatenate([grad_short, head_rows], axis=1)
    grad_qkv = (
        short_weight[:, 0, None, :] * extended_grad[:, :-2, :]
        + short_weight[:, 1, None, :] * extended_grad[:, 1:-1, :]
        + short_weight[:, 2, None, :] * extended_grad[:, 2:, :]
    ).astype(jnp.bfloat16)
    return (output, grad_qkv, grad_filter)


def solution(mesh):
    in_specs = (
        P(None, "seq", "ch"),
        P("seq", "ch"),
        P("ch"),
        P(None, None, "ch"),
        P(None, "ch"),
        P("seq", "ch"),
    )
    out_specs = (P("seq", "ch"), P(None, "seq", "ch"), P("seq", "ch"))
    return jax.shard_map(local, mesh=mesh, in_specs=in_specs, out_specs=out_specs, check_vma=False)
```

profile of v0, /device:TPU:1, one launch (start us, length us, event | category | flops | bytes accessed | tf_op | source)
XLA Modules:
  0.0 649.4 jit_solution(5705717059407092852)
XLA Ops:
  0.7 5.0 all-to-all-start.6
  6.4 4.4 collective-permute-start
  10.8 24.7 %all_gather.7 = bf16[128,2048]{1,0:T(8,128)(2,1)S(1)} all-gather(bf16[128,512]{1,0:T(8,128)(2,1)S(1)} %copy-done.18), channel_id=1, replica_groups=mesh['seq'=128,'ch'=4] {'ch'}, dimensions={1}, use_global_device_ids=true | all-gather | bytes 655360 | tf_op jit(solution)/shard_map/all_gather | solution.py:114
  35.5 1.6 multiply_add_fusion
  37.1 2.4 copy.51
  39.5 2.1 fusion.230
  42.7 24.8 %all-to-all-start.7 = ((f32[1,128,512]{2,0,1:T(1,128)}), f32[1,128,512]{2,0,1:T(1,128)S(1)}, u32[]{:S(2)}, u32[]{:S(2)}) async-start(f32[1,128,512]{2,0,1:T(1,128)} %copy.52), calls=%async_computation.7 | async-start | bytes 524288 | tf_op jit(solution)/shard_map/all_to_all | solution.py:35
  67.5 1.3 copy.43
  68.9 21.0 %all-to-all-done.7 = f32[1,128,512]{2,0,1:T(1,128)S(1)} async-done(((f32[1,128,512]{2,0,1:T(1,128)}), f32[1,128,512]{2,0,1:T(1,128)S(1)}, u32[]{:S(2)}, u32[]{:S(2)}) %all-to-all-start.7) | async-done | bytes 262176 | tf_op jit(solution)/shard_map/all_to_all | solution.py:35
  89.9 7.4 %all-to-all-start = ((f32[1,128,1024]{2,0,1:T(1,128)}), f32[1,128,1024]{2,0,1:T(1,128)S(1)}, u32[]{:S(2)}, u32[]{:S(2)}) async-start(f32[1,128,1024]{2,0,1:T(1,128)} %copy.43), calls=%async_computation | async-start | bytes 1048576 | tf_op jit(solution)/shard_map/all_to_all | solution.py:35
  98.4 1.2 subtract_bitcast_fusion.2
  99.5 1.3 copy.53
  100.9 29.7 %all-to-all-done = f32[1,128,1024]{2,0,1:T(1,128)S(1)} async-done(((f32[1,128,1024]{2,0,1:T(1,128)}), f32[1,128,1024]{2,0,1:T(1,128)S(1)}, u32[]{:S(2)}, u32[]{:S(2)}) %all-to-all-start) | async-done | bytes 524320 | tf_op jit(solution)/shard_map/all_to_all | solution.py:35
  130.6 7.1 %all-to-all-start.8 = ((f32[256,1,512]{2,1,0:T(1,128)}), f32[256,1,512]{2,1,0:T(1,128)S(1)}, u32[]{:S(2)}, u32[]{:S(2)}) async-start(f32[256,1,512]{2,1,0:T(1,128)} %copy.53), calls=%async_computation.8 | async-start | bytes 1048576 | tf_op jit(solution)/shard_map/all_to_all | solution.py:47
  137.7 1.3 copy.55
  139.1 31.9 %all-to-all-done.8 = f32[256,1,512]{2,1,0:T(1,128)S(1)} async-done(((f32[256,1,512]{2,1,0:T(1,128)}), f32[256,1,512]{2,1,0:T(1,128)S(1)}, u32[]{:S(2)}, u32[]{:S(2)}) %all-to-all-start.8) | async-done | bytes 524320 | tf_op jit(solution)/shard_map/all_to_all | solution.py:47
  170.9 7.6 %all-to-all-start.9 = ((f32[256,1,512]{2,1,0:T(1,128)}), f32[256,1,512]{2,1,0:T(1,128)S(1)}, u32[]{:S(2)}, u32[]{:S(2)}) async-start(f32[256,1,512]{2,1,0:T(1,128)} %copy.55), calls=%async_computation.9 | async-start | bytes 1048576 | tf_op jit(solution)/shard_map/all_to_all | solution.py:48
  178.5 1.5 convolution_negate_fusion
  180.0 1.7 add_bitcast_fusion.1
  181.7 2.1 copy.44
  183.8 27.9 %all-to-all-done.9 = f32[256,1,512]{2,1,0:T(1,128)S(1)} async-done(((f32[256,1,512]{2,1,0:T(1,128)}), f32[256,1,512]{2,1,0:T(1,128)S(1)}, u32[]{:S(2)}, u32[]{:S(2)}) %all-to-all-start.9) | async-done | bytes 524320 | tf_op jit(solution)/shard_map/all_to_all | solution.py:48
  211.7 7.6 %all-to-all-start.1 = ((f32[256,1,1024]{2,1,0:T(1,128)}), f32[256,1,1024]{2,1,0:T(1,128)}, u32[]{:S(2)}, u32[]{:S(2)}) async-start(f32[256,1,1024]{2,1,0:T(1,128)} %copy.44), calls=%async_computation.1 | async-start | bytes 2097152 | tf_op jit(solution)/shard_map/all_to_all | solution.py:47
  219.3 2.1 copy.46
  221.4 51.9 %all-to-all-done.1 = f32[256,1,1024]{2,1,0:T(1,128)} async-done(((f32[256,1,1024]{2,1,0:T(1,128)}), f32[256,1,1024]{2,1,0:T(1,128)}, u32[]{:S(2)}, u32[]{:S(2)}) %all-to-all-start.1) | async-done | bytes 1048608 | tf_op jit(solution)/shard_map/all_to_all | solution.py:47
  273.4 8.8 %all-to-all-start.2 = ((f32[256,1,1024]{2,1,0:T(1,128)}), f32[256,1,1024]{2,1,0:T(1,128)S(1)}, u32[]{:S(2)}, u32[]{:S(2)}) async-start(f32[256,1,1024]{2,1,0:T(1,128)} %copy.46), calls=%async_computation.2 | async-start | bytes 2097152 | tf_op jit(solution)/shard_map/all_to_all | solution.py:48
  284.0 1.6 fusion.25
  285.6 1.6 fusion.5
  287.2 2.3 copy.45
  289.6 2.2 fusion.9
  291.8 44.7 %all-to-all-done.2 = f32[256,1,1024]{2,1,0:T(1,128)S(1)} async-done(((f32[256,1,1024]{2,1,0:T(1,128)}), f32[256,1,1024]{2,1,0:T(1,128)S(1)}, u32[]{:S(2)}, u32[]{:S(2)}) %all-to-all-start.2) | async-done | bytes 1048608 | tf_op jit(solution)/shard_map/all_to_all | solution.py:48
  337.5 2.3 copy.47
  339.9 1.2 fusion.11
  341.1 1.2 fusion.1
  342.4 1.2 fusion
  343.7 1.9 multiply_add_fusion.2
  348.1 1.9 add_bitcast_fusion.3
  349.9 2.0 copy.48
  352.0 9.4 %all-to-all-start.3 = ((f32[2,128,512]{2,0,1:T(2,128)}), f32[2,128,512]{2,0,1:T(2,128)}, u32[]{:S(2)}, u32[]{:S(2)}) async-start(f32[2,128,512]{2,0,1:T(2,128)} %copy.48), calls=%async_computation.3 | async-start | bytes 1048576 | tf_op jit(solution)/shard_map/all_to_all | solution.py:75
  361.4 1.2 fusion.15
  362.6 1.2 fusion.14
  363.9 1.2 convolution_add_fusion
  365.1 2.4 add_bitcast_fusion
  367.5 2.3 copy.57
  369.7 24.3 %all-to-all-done.3 = f32[2,128,512]{2,0,1:T(2,128)} async-done(((f32[2,128,512]{2,0,1:T(2,128)}), f32[2,128,512]{2,0,1:T(2,128)}, u32[]{:S(2)}, u32[]{:S(2)}) %all-to-all-start.3) | async-done | bytes 524320 | tf_op jit(solution)/shard_map/all_to_all | solution.py:75
  394.1 7.1 %all-to-all-start.10 = ((f32[2,128,1024]{2,0,1:T(2,128)}), f32[2,128,1024]{2,0,1:T(2,128)S(1)}, u32[]{:S(2)}, u32[]{:S(2)}) async-start(f32[2,128,1024]{2,0,1:T(2,128)} %copy.57), calls=%async_computation.10 | async-start | bytes 2097152 | tf_op jit(solution)/shard_map/all_to_all | solution.py:75
  401.2 1.3 copy.58
  402.5 53.1 %all-to-all-done.10 = f32[2,128,1024]{2,0,1:T(2,128)S(1)} async-done(((f32[2,128,1024]{2,0,1:T(2,128)}), f32[2,128,1024]{2,0,1:T(2,128)S(1)}, u32[]{:S(2)}, u32[]{:S(2)}) %all-to-all-start.10) | async-done | bytes 1048608 | tf_op jit(solution)/shard_map/all_to_all | solution.py:75
  455.6 8.4 %all-to-all-start.11 = ((f32[2,128,1024]{2,0,1:T(2,128)}), f32[2,128,1024]{2,0,1:T(2,128)S(1)}, u32[]{:S(2)}, u32[]{:S(2)}) async-start(f32[2,128,1024]{2,0,1:T(2,128)} %copy.58), calls=%async_computation.11 | async-start | bytes 2097152 | tf_op jit(solution)/shard_map/all_to_all | solution.py:76
  465.0 53.4 %all-to-all-done.11 = f32[2,128,1024]{2,0,1:T(2,128)S(1)} async-done(((f32[2,128,1024]{2,0,1:T(2,128)}), f32[2,128,1024]{2,0,1:T(2,128)S(1)}, u32[]{:S(2)}, u32[]{:S(2)}) %all-to-all-start.11) | async-done | bytes 1048608 | tf_op jit(solution)/shard_map/all_to_all | solution.py:76
  518.4 8.7 %all-to-all-start.4 = ((f32[2,128,512]{2,0,1:T(2,128)}), f32[2,128,512]{2,0,1:T(2,128)S(1)}, u32[]{:S(2)}, u32[]{:S(2)}) async-start(f32[2,128,512]{2,0,1:T(2,128)} %copy.49), calls=%async_computation.4 | async-start | bytes 1048576 | tf_op jit(solution)/shard_map/all_to_all | solution.py:76
  527.1 1.7 reshape.170
  528.8 1.7 reshape.171
  530.6 1.2 fusion.82
  531.8 1.2 fusion.3
  533.0 1.3 copy.59
  534.3 25.9 %all-to-all-done.4 = f32[2,128,512]{2,0,1:T(2,128)S(1)} async-done(((f32[2,128,512]{2,0,1:T(2,128)}), f32[2,128,512]{2,0,1:T(2,128)S(1)}, u32[]{:S(2)}, u32[]{:S(2)}) %all-to-all-start.4) | async-done | bytes 524320 | tf_op jit(solution)/shard_map/all_to_all | solution.py:76
  560.2 7.1 %all-to-all-start.12 = ((f32[128,1,1024]{2,1,0:T(1,128)}), f32[128,1,1024]{2,1,0:T(1,128)S(1)}, u32[]{:S(2)}, u32[]{:S(2)}) async-start(f32[128,1,1024]{2,1,0:T(1,128)} %copy.59), calls=%async_computation.12 | async-start | bytes 1048576 | tf_op jit(solution)/shard_map/all_to_all | solution.py:81
  567.3 1.4 reshape.167
  572.0 28.5 %all-to-all-done.12 = f32[128,1,1024]{2,1,0:T(1,128)S(1)} async-done(((f32[128,1,1024]{2,1,0:T(1,128)}), f32[128,1,1024]{2,1,0:T(1,128)S(1)}, u32[]{:S(2)}, u32[]{:S(2)}) %all-to-all-start.12) | async-done | bytes 524320 | tf_op jit(solution)/shard_map/all_to_all | solution.py:81
  600.5 7.1 %all-to-all-start.5 = ((f32[128,1,512]{2,1,0:T(1,128)}), f32[128,1,512]{2,1,0:T(1,128)S(1)}, u32[]{:S(2)}, u32[]{:S(2)}) async-start(f32[128,1,512]{2,1,0:T(1,128)} %copy.50), calls=%async_computation.5 | async-start | bytes 524288 | tf_op jit(solution)/shard_map/all_to_all | solution.py:81
  607.8 22.3 %all-to-all-done.5 = f32[128,1,512]{2,1,0:T(1,128)S(1)} async-done(((f32[128,1,512]{2,1,0:T(1,128)}), f32[128,1,512]{2,1,0:T(1,128)S(1)}, u32[]{:S(2)}, u32[]{:S(2)}) %all-to-all-start.5) | async-done | bytes 262176 | tf_op jit(solution)/shard_map/all_to_all | solution.py:81
  631.1 4.3 collective-permute-start.1
  635.4 11.6 %all_gather.6 = bf16[128,2048]{1,0:T(8,128)(2,1)S(1)} all-gather(bf16[128,512]{1,0:T(8,128)(2,1)S(1)} %get-tuple-element.19), channel_id=1, replica_groups=mesh['seq'=128,'ch'=4] {'ch'}, dimensions={1}, use_global_device_ids=true | all-gather | bytes 655360 | tf_op jit(solution)/shard_map/all_gather | solution.py:109
  647.0 1.1 convolution_convert_fusion
  (74 shorter events, 14.7 us)
Async XLA Ops:
  0.6 10.1 %copy-start.19 = (f32[3,3,512]{2,1,0:T(4,128)S(1)}, f32[3,3,512]{2,1,0:T(4,128)}, u32[]{:S(2)}) copy-start(f32[3,3,512]{2,1,0:T(4,128)} %param.9) | copy-start | bytes 55300
  0.6 10.2 %copy-start.18 = (bf16[128,512]{1,0:T(8,128)(2,1)S(1)}, bf16[128,512]{1,0:T(8,128)(2,1)}, u32[]{:S(2)}) copy-start(bf16[128,512]{1,0:T(8,128)(2,1)} %param.11) | copy-start | bytes 393220
  0.7 36.4 %all-to-all-start.6 = ((bf16[4,512,512]{2,1,0:T(8,128)(2,1)}), bf16[4,512,512]{2,1,0:T(8,128)(2,1)S(1)}, u32[]{:S(2)}, u32[]{:S(2)}) async-start(bf16[4,512,512]{2,1,0:T(8,128)(2,1)} %bitcast.200), calls=%async_computation.6 | async-start | bytes 4194304 | tf_op jit(solution)/shard_map/all_to_all | solution.py:115
  6.4 29.1 %collective-permute-start = (bf16[3,2,512]{2,1,0:T(2,128)(2,1)S(1)}, bf16[3,2,512]{2,1,0:T(2,128)(2,1)S(1)}, u32[]{:S(2)}, u32[]{:S(2)}) collective-permute-start(bf16[3,2,512]{2,1,0:T(2,128)(2,1)S(1)} %slice.59), channel_id=1, source_target_pairs={{0,4},{4,8},{8,12},{12,16},{16,20},{20,24},{24,28},{28,32},{32,36}... | collective-permute-start | bytes 18440 | tf_op jit(solution)/shard_map/ppermute | solution.py:14
  39.5 28.0 %copy-start.17 = (f32[128,512]{1,0:T(8,128)S(1)}, f32[128,512]{1,0:T(8,128)}, u32[]{:S(2)}) copy-start(f32[128,512]{1,0:T(8,128)} %param.7) | copy-start | bytes 786436
  41.6 27.3 %copy-start.8 = (f32[128,512]{1,0:T(8,128)}, f32[128,512]{1,0:T(8,128)S(1)}, u32[]{:S(2)}) copy-start(f32[128,512]{1,0:T(8,128)S(1)} %fusion.230) | copy-start | bytes 786436
  41.7 48.2 %copy-start.6 = (f32[128,512]{1,0:T(8,128)}, f32[128,512]{1,0:T(8,128)S(1)}, u32[]{:S(2)}) copy-start(f32[128,512]{1,0:T(8,128)S(1)} %get-tuple-element.22) | copy-start | bytes 786436
  42.7 47.2 %all-to-all-start.7 = ((f32[1,128,512]{2,0,1:T(1,128)}), f32[1,128,512]{2,0,1:T(1,128)S(1)}, u32[]{:S(2)}, u32[]{:S(2)}) async-start(f32[1,128,512]{2,0,1:T(1,128)} %copy.52), calls=%async_computation.7 | async-start | bytes 524288 | tf_op jit(solution)/shard_map/all_to_all | solution.py:35
  89.9 40.7 %all-to-all-start = ((f32[1,128,1024]{2,0,1:T(1,128)}), f32[1,128,1024]{2,0,1:T(1,128)S(1)}, u32[]{:S(2)}, u32[]{:S(2)}) async-start(f32[1,128,1024]{2,0,1:T(1,128)} %copy.43), calls=%async_computation | async-start | bytes 1048576 | tf_op jit(solution)/shard_map/all_to_all | solution.py:35
  130.6 40.3 %all-to-all-start.8 = ((f32[256,1,512]{2,1,0:T(1,128)}), f32[256,1,512]{2,1,0:T(1,128)S(1)}, u32[]{:S(2)}, u32[]{:S(2)}) async-start(f32[256,1,512]{2,1,0:T(1,128)} %copy.53), calls=%async_computation.8 | async-start | bytes 1048576 | tf_op jit(solution)/shard_map/all_to_all | solution.py:47
  170.9 10.8 %copy-start.10 = (f32[256,1,512]{2,1,0:T(1,128)}, f32[256,1,512]{2,1,0:T(1,128)S(1)}, u32[]{:S(2)}) copy-start(f32[256,1,512]{2,1,0:T(1,128)S(1)} %all-to-all-done.8) | copy-start | bytes 1572868
  170.9 40.8 %all-to-all-start.9 = ((f32[256,1,512]{2,1,0:T(1,128)}), f32[256,1,512]{2,1,0:T(1,128)S(1)}, u32[]{:S(2)}, u32[]{:S(2)}) async-start(f32[256,1,512]{2,1,0:T(1,128)} %copy.55), calls=%async_computation.9 | async-start | bytes 1048576 | tf_op jit(solution)/shard_map/all_to_all | solution.py:48
  211.7 9.7 %copy-start.12 = (f32[256,1,512]{2,1,0:T(1,128)}, f32[256,1,512]{2,1,0:T(1,128)S(1)}, u32[]{:S(2)}) copy-start(f32[256,1,512]{2,1,0:T(1,128)S(1)} %all-to-all-done.9) | copy-start | bytes 1572868
  211.7 61.7 %all-to-all-start.1 = ((f32[256,1,1024]{2,1,0:T(1,128)}), f32[256,1,1024]{2,1,0:T(1,128)}, u32[]{:S(2)}, u32[]{:S(2)}) async-start(f32[256,1,1024]{2,1,0:T(1,128)} %copy.44), calls=%async_computation.1 | async-start | bytes 2097152 | tf_op jit(solution)/shard_map/all_to_all | solution.py:47
  219.3 63.0 %copy-start.11 = (f32[256,1,512]{2,1,0:T(1,128)S(1)}, f32[256,1,512]{2,1,0:T(1,128)}, u32[]{:S(2)}) copy-start(f32[256,1,512]{2,1,0:T(1,128)} %copy-done.10) | copy-start | bytes 1572868
  273.4 9.4 %copy-start.13 = (f32[256,1,512]{2,1,0:T(1,128)S(1)}, f32[256,1,512]{2,1,0:T(1,128)}, u32[]{:S(2)}) copy-start(f32[256,1,512]{2,1,0:T(1,128)} %copy-done.12) | copy-start | bytes 1572868
  273.4 63.1 %all-to-all-start.2 = ((f32[256,1,1024]{2,1,0:T(1,128)}), f32[256,1,1024]{2,1,0:T(1,128)S(1)}, u32[]{:S(2)}, u32[]{:S(2)}) async-start(f32[256,1,1024]{2,1,0:T(1,128)} %copy.46), calls=%async_computation.2 | async-start | bytes 2097152 | tf_op jit(solution)/shard_map/all_to_all | solution.py:48
  336.5 1.0 copy-start.3
  339.9 1.2 copy-start.2
  342.4 1.3 copy-start.15
  342.4 1.3 copy-start.16
  348.1 13.3 %copy-start.1 = (f32[2,128,512]{1,2,0:T(8,128)S(1)}, f32[2,128,512]{1,2,0:T(8,128)}, u32[]{:S(2)}) copy-start(f32[2,128,512]{1,2,0:T(8,128)} %get-tuple-element.8) | copy-start | bytes 1572868
  352.0 42.1 %all-to-all-start.3 = ((f32[2,128,512]{2,0,1:T(2,128)}), f32[2,128,512]{2,0,1:T(2,128)}, u32[]{:S(2)}, u32[]{:S(2)}) async-start(f32[2,128,512]{2,0,1:T(2,128)} %copy.48), calls=%async_computation.3 | async-start | bytes 1048576 | tf_op jit(solution)/shard_map/all_to_all | solution.py:75
  394.1 61.5 %all-to-all-start.10 = ((f32[2,128,1024]{2,0,1:T(2,128)}), f32[2,128,1024]{2,0,1:T(2,128)S(1)}, u32[]{:S(2)}, u32[]{:S(2)}) async-start(f32[2,128,1024]{2,0,1:T(2,128)} %copy.57), calls=%async_computation.10 | async-start | bytes 2097152 | tf_op jit(solution)/shard_map/all_to_all | solution.py:75
  401.2 62.8 %copy-start.14 = (f32[2,128,512]{1,2,0:T(8,128)S(1)}, f32[2,128,512]{1,2,0:T(8,128)}, u32[]{:S(2)}) copy-start(f32[2,128,512]{1,2,0:T(8,128)} %get-tuple-element.17) | copy-start | bytes 1572868
  455.6 62.8 %all-to-all-start.11 = ((f32[2,128,1024]{2,0,1:T(2,128)}), f32[2,128,1024]{2,0,1:T(2,128)S(1)}, u32[]{:S(2)}, u32[]{:S(2)}) async-start(f32[2,128,1024]{2,0,1:T(2,128)} %copy.58), calls=%async_computation.11 | async-start | bytes 2097152 | tf_op jit(solution)/shard_map/all_to_all | solution.py:76
  518.4 41.8 %all-to-all-start.4 = ((f32[2,128,512]{2,0,1:T(2,128)}), f32[2,128,512]{2,0,1:T(2,128)S(1)}, u32[]{:S(2)}, u32[]{:S(2)}) async-start(f32[2,128,512]{2,0,1:T(2,128)} %copy.49), calls=%async_computation.4 | async-start | bytes 1048576 | tf_op jit(solution)/shard_map/all_to_all | solution.py:76
  528.8 1.7 copy-start.4
  530.6 1.2 copy-start.5
  560.2 40.3 %all-to-all-start.12 = ((f32[128,1,1024]{2,1,0:T(1,128)}), f32[128,1,1024]{2,1,0:T(1,128)S(1)}, u32[]{:S(2)}, u32[]{:S(2)}) async-start(f32[128,1,1024]{2,1,0:T(1,128)} %copy.59), calls=%async_computation.12 | async-start | bytes 1048576 | tf_op jit(solution)/shard_map/all_to_all | solution.py:81
  569.1 61.0 %copy-start.7 = (f32[128,512]{1,0:T(8,128)S(1)}, f32[128,512]{1,0:T(8,128)}, u32[]{:S(2)}) copy-start(f32[128,512]{1,0:T(8,128)} %copy-done.6) | copy-start | bytes 786436
  569.1 61.0 %copy-start.9 = (f32[128,512]{1,0:T(8,128)S(1)}, f32[128,512]{1,0:T(8,128)}, u32[]{:S(2)}) copy-start(f32[128,512]{1,0:T(8,128)} %copy-done.8) | copy-start | bytes 786436
  569.1 61.0 %copy-start.20 = (f32[512]{0:T(512)S(1)}, f32[512]{0:T(512)}, u32[]{:S(2)}) copy-start(f32[512]{0:T(512)} %param.8) | copy-start | bytes 6148
  600.5 29.5 %all-to-all-start.5 = ((f32[128,1,512]{2,1,0:T(1,128)}), f32[128,1,512]{2,1,0:T(1,128)S(1)}, u32[]{:S(2)}, u32[]{:S(2)}) async-start(f32[128,1,512]{2,1,0:T(1,128)} %copy.50), calls=%async_computation.5 | async-start | bytes 524288 | tf_op jit(solution)/shard_map/all_to_all | solution.py:81
  631.0 16.0 %copy-start = (bf16[2048,512]{1,0:T(8,128)(2,1)S(1)}, bf16[2048,512]{1,0:T(8,128)(2,1)}, u32[]{:S(2)}) copy-start(bf16[2048,512]{1,0:T(8,128)(2,1)} %param.10) | copy-start | bytes 6291460
  631.1 17.0 %collective-permute-start.1 = (f32[3,2,512]{2,1,0:T(2,128)S(1)}, f32[3,2,512]{2,1,0:T(2,128)S(1)}, u32[]{:S(2)}, u32[]{:S(2)}) collective-permute-start(f32[3,2,512]{2,1,0:T(2,128)S(1)} %slice.85), channel_id=1, source_target_pairs={{4,0},{8,4},{12,8},{16,12},{20,16},{24,20},{28,24},{32,28},{36,32}... | collective-permute-start | bytes 36872 | tf_op jit(solution)/shard_map/ppermute | solution.py:14
where the time goes:
time: 659 us; the launch traced here: 649 us
  waiting for transfers between devices  415 us (63%)
  starting transfers between devices  125 us (19%)
  blocking collectives  36.3 us (6%)
  matrix products  35.1 us (5%)
  local copies, waits for them, and re-layouts  33.2 us (5%)
    all_to_all x2, waiting for transfers between devices, forward_spectrum(): lax.all_to_all(turned_re, 'seq', split_axis=0, concat_axis=1, tiled=True)  83.8 us
    all_to_all x2, waiting for transfers between devices, time_signal(): lax.all_to_all(turned_im, 'seq', split_axis=1, concat_axis=0, tiled=True)  79.3 us
    all_to_all x2, waiting for transfers between devices, time_signal(): lax.all_to_all(turned_re, 'seq', split_axis=1, concat_axis=0, tiled=True)  77.4 us
    all_to_all x2, waiting for transfers between devices, forward_spectrum(): lax.all_to_all(turned_im, 'seq', split_axis=0, concat_axis=1, tiled=True)  72.7 us
    all_to_all x2, waiting for transfers between devices, time_signal(): lax.all_to_all(returned, 'seq', split_axis=0, concat_axis=1, tiled=True)[0]  50.8 us
    all_to_all x2, waiting for transfers between devices, forward_spectrum(): lax.all_to_all(signal[None], 'seq', split_axis=1, concat_axis=0, tiled=True)  50.7 us
    all_to_all x2, starting transfers between devices, forward_spectrum(): lax.all_to_all(signal[None], 'seq', split_axis=1, concat_axis=0, tiled=True)  32.2 us
    dot_general x24, matrix products, contract(): jnp.einsum(pattern, matrix, values, precision=HIGHEST, preferred_element_...  32 us
  transfers between devices with their start and end apart: 15, of which 12 were waited for; matrix products, arithmetic and copies ran while one was open for 8% of the time, Pallas kernels for 0%

commit v1 on v0

--- a/solution.py
+++ b/solution.py
@@ -111,7 +111,9 @@
         preferred_element_type=jnp.float32,
     )
     output = projected.astype(jnp.bfloat16)
-    grad_all = lax.all_gather(g_out, "ch", axis=1, tiled=True)
+    grad_all = jnp.concatenate(
+        lax.all_to_all(jnp.stack([g_out] * lax.axis_size("ch")), "ch", 0, 0), axis=1
+    )
     rows_all = lax.all_to_all(w_out, "ch", split_axis=0, concat_axis=1, tiled=True)
     grad_gated = lax.dot_general(
         grad_all, rows_all, (((1,), (1,)), ((), ())), preferred_element_type=jnp.float32

time: 659 us -> 658 us (level)
  blocking collectives: 36.3 us -> 23.2 us
  waiting for transfers between devices: 415 us -> 425 us
    all_gather x1 -> x0, blocking collectives: 24.7 us -> none  [local(): grad_all = lax.all_gather(g_out, 'ch', axis=1, tiled=True)]
    all_to_all x0 -> x1, blocking collectives: none -> 11.6 us  [local(): lax.all_to_all(jnp.stack([g_out] * lax.axis_size('ch')), 'ch', 0, 0)]
    all_to_all x1, waiting for transfers between devices: 0.01 us -> 10.3 us  [local(): lax.all_to_all(w_out, 'ch', split_axis=0, concat_axis=1, tiled=True)]
  transfers between devices with their start and end apart: 15 -> 15, of which waited for: 12 -> 14; matrix products, arithmetic and copies ran while one was open for 8% -> 8% of each run, Pallas kernels for 0% -> 0%
where the time goes in v1:
time: 658 us; the launch traced here: 648 us
  waiting for transfers between devices  425 us (65%)
  starting transfers between devices  129 us (20%)
  matrix products  33.8 us (5%)
  local copies, waits for them, and re-layouts  31.5 us (5%)
  blocking collectives  23.2 us (4%)
    all_to_all x2, waiting for transfers between devices, forward_spectrum(): lax.all_to_all(turned_re, 'seq', split_axis=0, concat_axis=1, tiled=True)  83.8 us
    all_to_all x2, waiting for transfers between devices, time_signal(): lax.all_to_all(turned_im, 'seq', split_axis=1, concat_axis=0, tiled=True)  79.3 us
    all_to_all x2, waiting for transfers between devices, time_signal(): lax.all_to_all(turned_re, 'seq', split_axis=1, concat_axis=0, tiled=True)  77.4 us
    all_to_all x2, waiting for transfers between devices, forward_spectrum(): lax.all_to_all(turned_im, 'seq', split_axis=0, concat_axis=1, tiled=True)  72.4 us
    all_to_all x2, waiting for transfers between devices, time_signal(): lax.all_to_all(returned, 'seq', split_axis=0, concat_axis=1, tiled=True)[0]  50.8 us
    all_to_all x2, waiting for transfers between devices, forward_spectrum(): lax.all_to_all(signal[None], 'seq', split_axis=1, concat_axis=0, tiled=True)  50.7 us
    all_to_all x2, starting transfers between devices, forward_spectrum(): lax.all_to_all(signal[None], 'seq', split_axis=1, concat_axis=0, tiled=True)  35 us
    dot_general x24, matrix products, contract(): jnp.einsum(pattern, matrix, values, precision=HIGHEST, preferred_element_...  31.9 us
  transfers between devices with their start and end apart: 15, of which 14 were waited for; matrix products, arithmetic and copies ran while one was open for 8% of the time, Pallas kernels for 0%

profile of v1, /device:TPU:1, one launch (start us, length us, event | category | flops | bytes accessed | tf_op | source)
XLA Modules:
  0.0 648.1 jit_solution(13509799022857387967)
XLA Ops:
  1.6 11.6 %all_to_all.189 = bf16[4,128,512]{2,1,0:T(8,128)(2,1)S(1)} all-to-all(bf16[4,128,512]{2,1,0:T(8,128)(2,1)S(1)} %stack.19), channel_id=1, replica_groups=mesh['seq'=128,'ch'=4] {'ch'}, dimensions={0} | all-to-all | bytes 1048576 | tf_op jit(solution)/shard_map/all_to_all | solution.py:115
  13.1 3.7 all-to-all-start.7
  17.6 6.9 %collective-permute-start = (bf16[3,2,512]{2,1,0:T(2,128)(2,1)S(1)}, bf16[3,2,512]{2,1,0:T(2,128)(2,1)S(1)}, u32[]{:S(2)}, u32[]{:S(2)}) collective-permute-start(bf16[3,2,512]{2,1,0:T(2,128)(2,1)S(1)} %slice.59), channel_id=1, source_target_pairs={{0,4},{4,8},{8,12},{12,16},{16,20},{20,24},{24,28},{28,32},{32,36}... | collective-permute-start | bytes 18440 | tf_op jit(solution)/shard_map/ppermute | solution.py:14
  25.3 1.6 multiply_add_fusion
  26.9 10.3 %all-to-all-done.7 = bf16[4,512,512]{2,1,0:T(8,128)(2,1)S(1)} async-done(((bf16[4,512,512]{2,1,0:T(8,128)(2,1)}), bf16[4,512,512]{2,1,0:T(8,128)(2,1)S(1)}, u32[]{:S(2)}, u32[]{:S(2)}) %all-to-all-start.7) | async-done | bytes 2097184 | tf_op jit(solution)/shard_map/all_to_all | solution.py:117
  39.8 27.7 %all-to-all-start.8 = ((f32[1,128,512]{2,0,1:T(1,128)}), f32[1,128,512]{2,0,1:T(1,128)S(1)}, u32[]{:S(2)}, u32[]{:S(2)}) async-start(f32[1,128,512]{2,0,1:T(1,128)} %copy.41), calls=%async_computation.8 | async-start | bytes 524288 | tf_op jit(solution)/shard_map/all_to_all | solution.py:35
  67.5 1.3 copy.33
  68.9 21.0 %all-to-all-done.8 = f32[1,128,512]{2,0,1:T(1,128)S(1)} async-done(((f32[1,128,512]{2,0,1:T(1,128)}), f32[1,128,512]{2,0,1:T(1,128)S(1)}, u32[]{:S(2)}, u32[]{:S(2)}) %all-to-all-start.8) | async-done | bytes 262176 | tf_op jit(solution)/shard_map/all_to_all | solution.py:35
  89.9 7.4 %all-to-all-start = ((f32[1,128,1024]{2,0,1:T(1,128)}), f32[1,128,1024]{2,0,1:T(1,128)S(1)}, u32[]{:S(2)}, u32[]{:S(2)}) async-start(f32[1,128,1024]{2,0,1:T(1,128)} %copy.33), calls=%async_computation | async-start | bytes 1048576 | tf_op jit(solution)/shard_map/all_to_all | solution.py:35
  97.3 1.1 convolution_negate_fusion.1
  98.4 1.2 subtract_bitcast_fusion.2
  99.5 1.3 copy.42
  100.9 29.7 %all-to-all-done = f32[1,128,1024]{2,0,1:T(1,128)S(1)} async-done(((f32[1,128,1024]{2,0,1:T(1,128)}), f32[1,128,1024]{2,0,1:T(1,128)S(1)}, u32[]{:S(2)}, u32[]{:S(2)}) %all-to-all-start) | async-done | bytes 524320 | tf_op jit(solution)/shard_map/all_to_all | solution.py:35
  130.6 7.1 %all-to-all-start.9 = ((f32[256,1,512]{2,1,0:T(1,128)}), f32[256,1,512]{2,1,0:T(1,128)S(1)}, u32[]{:S(2)}, u32[]{:S(2)}) async-start(f32[256,1,512]{2,1,0:T(1,128)} %copy.42), calls=%async_computation.9 | async-start | bytes 1048576 | tf_op jit(solution)/shard_map/all_to_all | solution.py:47
  137.7 1.3 copy.44
  139.1 31.9 %all-to-all-done.9 = f32[256,1,512]{2,1,0:T(1,128)S(1)} async-done(((f32[256,1,512]{2,1,0:T(1,128)}), f32[256,1,512]{2,1,0:T(1,128)S(1)}, u32[]{:S(2)}, u32[]{:S(2)}) %all-to-all-start.9) | async-done | bytes 524320 | tf_op jit(solution)/shard_map/all_to_all | solution.py:47
  170.9 7.1 %all-to-all-start.10 = ((f32[256,1,512]{2,1,0:T(1,128)}), f32[256,1,512]{2,1,0:T(1,128)S(1)}, u32[]{:S(2)}, u32[]{:S(2)}) async-start(f32[256,1,512]{2,1,0:T(1,128)} %copy.44), calls=%async_computation.10 | async-start | bytes 1048576 | tf_op jit(solution)/shard_map/all_to_all | solution.py:48
  178.1 1.5 convolution_negate_fusion
  179.6 1.7 add_bitcast_fusion.1
  181.3 2.1 copy.34
  183.3 27.9 %all-to-all-done.10 = f32[256,1,512]{2,1,0:T(1,128)S(1)} async-done(((f32[256,1,512]{2,1,0:T(1,128)}), f32[256,1,512]{2,1,0:T(1,128)S(1)}, u32[]{:S(2)}, u32[]{:S(2)}) %all-to-all-start.10) | async-done | bytes 524320 | tf_op jit(solution)/shard_map/all_to_all | solution.py:48
  211.3 7.6 %all-to-all-start.1 = ((f32[256,1,1024]{2,1,0:T(1,128)}), f32[256,1,1024]{2,1,0:T(1,128)}, u32[]{:S(2)}, u32[]{:S(2)}) async-start(f32[256,1,1024]{2,1,0:T(1,128)} %copy.34), calls=%async_computation.1 | async-start | bytes 2097152 | tf_op jit(solution)/shard_map/all_to_all | solution.py:47
  218.9 2.1 copy.36
  221.0 52.0 %all-to-all-done.1 = f32[256,1,1024]{2,1,0:T(1,128)} async-done(((f32[256,1,1024]{2,1,0:T(1,128)}), f32[256,1,1024]{2,1,0:T(1,128)}, u32[]{:S(2)}, u32[]{:S(2)}) %all-to-all-start.1) | async-done | bytes 1048608 | tf_op jit(solution)/shard_map/all_to_all | solution.py:47
  272.9 9.0 %all-to-all-start.2 = ((f32[256,1,1024]{2,1,0:T(1,128)}), f32[256,1,1024]{2,1,0:T(1,128)}, u32[]{:S(2)}, u32[]{:S(2)}) async-start(f32[256,1,1024]{2,1,0:T(1,128)} %copy.36), calls=%async_computation.2 | async-start | bytes 2097152 | tf_op jit(solution)/shard_map/all_to_all | solution.py:48
  283.7 1.6 fusion.30
  285.3 1.6 fusion.7
  286.9 2.3 copy.35
  289.3 2.2 fusion.14
  291.5 44.5 %all-to-all-done.2 = f32[256,1,1024]{2,1,0:T(1,128)} async-done(((f32[256,1,1024]{2,1,0:T(1,128)}), f32[256,1,1024]{2,1,0:T(1,128)}, u32[]{:S(2)}, u32[]{:S(2)}) %all-to-all-start.2) | async-done | bytes 1048608 | tf_op jit(solution)/shard_map/all_to_all | solution.py:48
  336.0 2.5 copy.37
  338.5 1.2 fusion.16
  339.7 1.2 fusion.3
  341.0 1.2 fusion.2
  342.3 1.9 multiply_add_fusion.2
  346.7 1.9 add_bitcast_fusion.3
  348.5 2.0 copy.38
  350.6 9.3 %all-to-all-start.3 = ((f32[2,128,512]{2,0,1:T(2,128)}), f32[2,128,512]{2,0,1:T(2,128)}, u32[]{:S(2)}, u32[]{:S(2)}) async-start(f32[2,128,512]{2,0,1:T(2,128)} %copy.38), calls=%async_computation.3 | async-start | bytes 1048576 | tf_op jit(solution)/shard_map/all_to_all | solution.py:75
  359.8 1.2 fusion.20
  361.1 1.2 fusion.19
  362.3 1.2 convolution_add_fusion
  363.6 2.3 add_bitcast_fusion
  365.9 2.3 copy.46
  368.2 24.4 %all-to-all-done.3 = f32[2,128,512]{2,0,1:T(2,128)} async-done(((f32[2,128,512]{2,0,1:T(2,128)}), f32[2,128,512]{2,0,1:T(2,128)}, u32[]{:S(2)}, u32[]{:S(2)}) %all-to-all-start.3) | async-done | bytes 524320 | tf_op jit(solution)/shard_map/all_to_all | solution.py:75
  392.5 7.1 %all-to-all-start.11 = ((f32[2,128,1024]{2,0,1:T(2,128)}), f32[2,128,1024]{2,0,1:T(2,128)S(1)}, u32[]{:S(2)}, u32[]{:S(2)}) async-start(f32[2,128,1024]{2,0,1:T(2,128)} %copy.46), calls=%async_computation.11 | async-start | bytes 2097152 | tf_op jit(solution)/shard_map/all_to_all | solution.py:75
  399.6 1.3 copy.47
  401.0 53.1 %all-to-all-done.11 = f32[2,128,1024]{2,0,1:T(2,128)S(1)} async-done(((f32[2,128,1024]{2,0,1:T(2,128)}), f32[2,128,1024]{2,0,1:T(2,128)S(1)}, u32[]{:S(2)}, u32[]{:S(2)}) %all-to-all-start.11) | async-done | bytes 1048608 | tf_op jit(solution)/shard_map/all_to_all | solution.py:75
  454.0 8.4 %all-to-all-start.12 = ((f32[2,128,1024]{2,0,1:T(2,128)}), f32[2,128,1024]{2,0,1:T(2,128)S(1)}, u32[]{:S(2)}, u32[]{:S(2)}) async-start(f32[2,128,1024]{2,0,1:T(2,128)} %copy.47), calls=%async_computation.12 | async-start | bytes 2097152 | tf_op jit(solution)/shard_map/all_to_all | solution.py:76
  463.4 53.4 %all-to-all-done.12 = f32[2,128,1024]{2,0,1:T(2,128)S(1)} async-done(((f32[2,128,1024]{2,0,1:T(2,128)}), f32[2,128,1024]{2,0,1:T(2,128)S(1)}, u32[]{:S(2)}, u32[]{:S(2)}) %all-to-all-start.12) | async-done | bytes 1048608 | tf_op jit(solution)/shard_map/all_to_all | solution.py:76
  516.8 8.8 %all-to-all-start.4 = ((f32[2,128,512]{2,0,1:T(2,128)}), f32[2,128,512]{2,0,1:T(2,128)S(1)}, u32[]{:S(2)}, u32[]{:S(2)}) async-start(f32[2,128,512]{2,0,1:T(2,128)} %copy.39), calls=%async_computation.4 | async-start | bytes 1048576 | tf_op jit(solution)/shard_map/all_to_all | solution.py:76
  525.6 1.7 reshape.177
  527.3 1.7 reshape.178
  529.0 1.2 fusion.88
  530.3 1.2 fusion.5
  531.5 1.3 copy.48
  532.8 25.9 %all-to-all-done.4 = f32[2,128,512]{2,0,1:T(2,128)S(1)} async-done(((f32[2,128,512]{2,0,1:T(2,128)}), f32[2,128,512]{2,0,1:T(2,128)S(1)}, u32[]{:S(2)}, u32[]{:S(2)}) %all-to-all-start.4) | async-done | bytes 524320 | tf_op jit(solution)/shard_map/all_to_all | solution.py:76
  558.7 7.1 %all-to-all-start.13 = ((f32[128,1,1024]{2,1,0:T(1,128)}), f32[128,1,1024]{2,1,0:T(1,128)S(1)}, u32[]{:S(2)}, u32[]{:S(2)}) async-start(f32[128,1,1024]{2,1,0:T(1,128)} %copy.48), calls=%async_computation.13 | async-start | bytes 1048576 | tf_op jit(solution)/shard_map/all_to_all | solution.py:81
  565.8 1.4 reshape.173
  570.5 28.5 %all-to-all-done.13 = f32[128,1,1024]{2,1,0:T(1,128)S(1)} async-done(((f32[128,1,1024]{2,1,0:T(1,128)}), f32[128,1,1024]{2,1,0:T(1,128)S(1)}, u32[]{:S(2)}, u32[]{:S(2)}) %all-to-all-start.13) | async-done | bytes 524320 | tf_op jit(solution)/shard_map/all_to_all | solution.py:81
  599.0 7.1 %all-to-all-start.5 = ((f32[128,1,512]{2,1,0:T(1,128)}), f32[128,1,512]{2,1,0:T(1,128)S(1)}, u32[]{:S(2)}, u32[]{:S(2)}) async-start(f32[128,1,512]{2,1,0:T(1,128)} %copy.40), calls=%async_computation.5 | async-start | bytes 524288 | tf_op jit(solution)/shard_map/all_to_all | solution.py:81
  606.3 22.3 %all-to-all-done.5 = f32[128,1,512]{2,1,0:T(1,128)S(1)} async-done(((f32[128,1,512]{2,1,0:T(1,128)}), f32[128,1,512]{2,1,0:T(1,128)S(1)}, u32[]{:S(2)}, u32[]{:S(2)}) %all-to-all-start.5) | async-done | bytes 262176 | tf_op jit(solution)/shard_map/all_to_all | solution.py:81
  629.6 4.3 collective-permute-start.1
  633.9 11.6 %all_gather.3 = bf16[128,2048]{1,0:T(8,128)(2,1)S(1)} all-gather(bf16[128,512]{1,0:T(8,128)(2,1)S(1)} %get-tuple-element.19), channel_id=1, replica_groups=mesh['seq'=128,'ch'=4] {'ch'}, dimensions={1}, use_global_device_ids=true | all-gather | bytes 655360 | tf_op jit(solution)/shard_map/all_gather | solution.py:109
  645.5 1.1 convolution_convert_fusion
  (66 shorter events, 15.7 us)
Async XLA Ops:
  13.1 11.4 %copy-start.15 = (f32[3,3,512]{2,1,0:T(4,128)S(1)}, f32[3,3,512]{2,1,0:T(4,128)}, u32[]{:S(2)}) copy-start(f32[3,3,512]{2,1,0:T(4,128)} %param.9) | copy-start | bytes 55300
  13.1 24.1 %all-to-all-start.7 = ((bf16[4,512,512]{2,1,0:T(8,128)(2,1)}), bf16[4,512,512]{2,1,0:T(8,128)(2,1)S(1)}, u32[]{:S(2)}, u32[]{:S(2)}) async-start(bf16[4,512,512]{2,1,0:T(8,128)(2,1)} %bitcast.206), calls=%async_computation.7 | async-start | bytes 4194304 | tf_op jit(solution)/shard_map/all_to_all | solution.py:117
  17.6 7.7 %collective-permute-start = (bf16[3,2,512]{2,1,0:T(2,128)(2,1)S(1)}, bf16[3,2,512]{2,1,0:T(2,128)(2,1)S(1)}, u32[]{:S(2)}, u32[]{:S(2)}) collective-permute-start(bf16[3,2,512]{2,1,0:T(2,128)(2,1)S(1)} %slice.59), channel_id=1, source_target_pairs={{0,4},{4,8},{8,12},{12,16},{16,20},{20,24},{24,28},{28,32},{32,36}... | collective-permute-start | bytes 18440 | tf_op jit(solution)/shard_map/ppermute | solution.py:14
  38.0 0.7 copy-start.7
  38.7 28.7 %copy-start.14 = (f32[128,512]{1,0:T(8,128)S(1)}, f32[128,512]{1,0:T(8,128)}, u32[]{:S(2)}) copy-start(f32[128,512]{1,0:T(8,128)} %param.7) | copy-start | bytes 786436
  38.8 51.0 %copy-start.5 = (f32[128,512]{1,0:T(8,128)}, f32[128,512]{1,0:T(8,128)S(1)}, u32[]{:S(2)}) copy-start(f32[128,512]{1,0:T(8,128)S(1)} %get-tuple-element.22) | copy-start | bytes 786436
  39.8 50.1 %all-to-all-start.8 = ((f32[1,128,512]{2,0,1:T(1,128)}), f32[1,128,512]{2,0,1:T(1,128)S(1)}, u32[]{:S(2)}, u32[]{:S(2)}) async-start(f32[1,128,512]{2,0,1:T(1,128)} %copy.41), calls=%async_computation.8 | async-start | bytes 524288 | tf_op jit(solution)/shard_map/all_to_all | solution.py:35
  89.9 40.7 %all-to-all-start = ((f32[1,128,1024]{2,0,1:T(1,128)}), f32[1,128,1024]{2,0,1:T(1,128)S(1)}, u32[]{:S(2)}, u32[]{:S(2)}) async-start(f32[1,128,1024]{2,0,1:T(1,128)} %copy.33), calls=%async_computation | async-start | bytes 1048576 | tf_op jit(solution)/shard_map/all_to_all | solution.py:35
  130.6 40.3 %all-to-all-start.9 = ((f32[256,1,512]{2,1,0:T(1,128)}), f32[256,1,512]{2,1,0:T(1,128)S(1)}, u32[]{:S(2)}, u32[]{:S(2)}) async-start(f32[256,1,512]{2,1,0:T(1,128)} %copy.42), calls=%async_computation.9 | async-start | bytes 1048576 | tf_op jit(solution)/shard_map/all_to_all | solution.py:47
  170.9 40.3 %all-to-all-start.10 = ((f32[256,1,512]{2,1,0:T(1,128)}), f32[256,1,512]{2,1,0:T(1,128)S(1)}, u32[]{:S(2)}, u32[]{:S(2)}) async-start(f32[256,1,512]{2,1,0:T(1,128)} %copy.44), calls=%async_computation.10 | async-start | bytes 1048576 | tf_op jit(solution)/shard_map/all_to_all | solution.py:48
  211.3 9.7 %copy-start.9 = (f32[256,1,512]{2,1,0:T(1,128)}, f32[256,1,512]{2,1,0:T(1,128)S(1)}, u32[]{:S(2)}) copy-start(f32[256,1,512]{2,1,0:T(1,128)S(1)} %all-to-all-done.10) | copy-start | bytes 1572868
  211.3 61.7 %all-to-all-start.1 = ((f32[256,1,1024]{2,1,0:T(1,128)}), f32[256,1,1024]{2,1,0:T(1,128)}, u32[]{:S(2)}, u32[]{:S(2)}) async-start(f32[256,1,1024]{2,1,0:T(1,128)} %copy.34), calls=%async_computation.1 | async-start | bytes 2097152 | tf_op jit(solution)/shard_map/all_to_all | solution.py:47
  272.9 9.5 %copy-start.10 = (f32[256,1,512]{2,1,0:T(1,128)S(1)}, f32[256,1,512]{2,1,0:T(1,128)}, u32[]{:S(2)}) copy-start(f32[256,1,512]{2,1,0:T(1,128)} %copy-done.9) | copy-start | bytes 1572868
  272.9 63.1 %all-to-all-start.2 = ((f32[256,1,1024]{2,1,0:T(1,128)}), f32[256,1,1024]{2,1,0:T(1,128)}, u32[]{:S(2)}, u32[]{:S(2)}) async-start(f32[256,1,1024]{2,1,0:T(1,128)} %copy.36), calls=%async_computation.2 | async-start | bytes 2097152 | tf_op jit(solution)/shard_map/all_to_all | solution.py:48
  338.5 1.2 copy-start.2
  341.0 1.3 copy-start.12
  341.0 1.3 copy-start.13
  346.7 13.2 %copy-start.1 = (f32[2,128,512]{1,2,0:T(8,128)S(1)}, f32[2,128,512]{1,2,0:T(8,128)}, u32[]{:S(2)}) copy-start(f32[2,128,512]{1,2,0:T(8,128)} %get-tuple-element.8) | copy-start | bytes 1572868
  350.6 42.0 %all-to-all-start.3 = ((f32[2,128,512]{2,0,1:T(2,128)}), f32[2,128,512]{2,0,1:T(2,128)}, u32[]{:S(2)}, u32[]{:S(2)}) async-start(f32[2,128,512]{2,0,1:T(2,128)} %copy.38), calls=%async_computation.3 | async-start | bytes 1048576 | tf_op jit(solution)/shard_map/all_to_all | solution.py:75
  392.5 61.5 %all-to-all-start.11 = ((f32[2,128,1024]{2,0,1:T(2,128)}), f32[2,128,1024]{2,0,1:T(2,128)S(1)}, u32[]{:S(2)}, u32[]{:S(2)}) async-start(f32[2,128,1024]{2,0,1:T(2,128)} %copy.46), calls=%async_computation.11 | async-start | bytes 2097152 | tf_op jit(solution)/shard_map/all_to_all | solution.py:75
  399.6 62.8 %copy-start.11 = (f32[2,128,512]{1,2,0:T(8,128)S(1)}, f32[2,128,512]{1,2,0:T(8,128)}, u32[]{:S(2)}) copy-start(f32[2,128,512]{1,2,0:T(8,128)} %get-tuple-element.17) | copy-start | bytes 1572868
  454.0 62.8 %all-to-all-start.12 = ((f32[2,128,1024]{2,0,1:T(2,128)}), f32[2,128,1024]{2,0,1:T(2,128)S(1)}, u32[]{:S(2)}, u32[]{:S(2)}) async-start(f32[2,128,1024]{2,0,1:T(2,128)} %copy.47), calls=%async_computation.12 | async-start | bytes 2097152 | tf_op jit(solution)/shard_map/all_to_all | solution.py:76
  516.8 41.9 %all-to-all-start.4 = ((f32[2,128,512]{2,0,1:T(2,128)}), f32[2,128,512]{2,0,1:T(2,128)S(1)}, u32[]{:S(2)}, u32[]{:S(2)}) async-start(f32[2,128,512]{2,0,1:T(2,128)} %copy.39), calls=%async_computation.4 | async-start | bytes 1048576 | tf_op jit(solution)/shard_map/all_to_all | solution.py:76
  527.3 1.7 copy-start.3
  529.0 1.2 copy-start.4
  558.7 40.3 %all-to-all-start.13 = ((f32[128,1,1024]{2,1,0:T(1,128)}), f32[128,1,1024]{2,1,0:T(1,128)S(1)}, u32[]{:S(2)}, u32[]{:S(2)}) async-start(f32[128,1,1024]{2,1,0:T(1,128)} %copy.48), calls=%async_computation.13 | async-start | bytes 1048576 | tf_op jit(solution)/shard_map/all_to_all | solution.py:81
  567.6 61.0 %copy-start.6 = (f32[128,512]{1,0:T(8,128)S(1)}, f32[128,512]{1,0:T(8,128)}, u32[]{:S(2)}) copy-start(f32[128,512]{1,0:T(8,128)} %copy-done.5) | copy-start | bytes 786436
  567.6 61.0 %copy-start.8 = (f32[128,512]{1,0:T(8,128)S(1)}, f32[128,512]{1,0:T(8,128)}, u32[]{:S(2)}) copy-start(f32[128,512]{1,0:T(8,128)} %copy-done.7) | copy-start | bytes 786436
  567.6 61.0 %copy-start.16 = (f32[512]{0:T(512)S(1)}, f32[512]{0:T(512)}, u32[]{:S(2)}) copy-start(f32[512]{0:T(512)} %param.8) | copy-start | bytes 6148
  599.0 29.5 %all-to-all-start.5 = ((f32[128,1,512]{2,1,0:T(1,128)}), f32[128,1,512]{2,1,0:T(1,128)S(1)}, u32[]{:S(2)}, u32[]{:S(2)}) async-start(f32[128,1,512]{2,1,0:T(1,128)} %copy.40), calls=%async_computation.5 | async-start | bytes 524288 | tf_op jit(solution)/shard_map/all_to_all | solution.py:81
  629.5 16.0 %copy-start = (bf16[2048,512]{1,0:T(8,128)(2,1)S(1)}, bf16[2048,512]{1,0:T(8,128)(2,1)}, u32[]{:S(2)}) copy-start(bf16[2048,512]{1,0:T(8,128)(2,1)} %param.10) | copy-start | bytes 6291460
  629.6 17.0 %collective-permute-start.1 = (f32[3,2,512]{2,1,0:T(2,128)S(1)}, f32[3,2,512]{2,1,0:T(2,128)S(1)}, u32[]{:S(2)}, u32[]{:S(2)}) collective-permute-start(f32[3,2,512]{2,1,0:T(2,128)S(1)} %slice.85), channel_id=1, source_target_pairs={{4,0},{8,4},{12,8},{16,12},{20,16},{24,20},{28,24},{32,28},{36,32}... | collective-permute-start | bytes 36872 | tf_op jit(solution)/shard_map/ppermute | solution.py:14
